TPU v7x, 256 devices: a whole 4x4x8 slice. The times are simulated.
256 devices in a mesh: context: 32 (over z, x), ulysses: 4 (over y), dp: 2 (over core).
Axes of the slice: x: 4, y: 4, z: 8, core: 2. Of those that a mesh axis runs over, the one named last changes fastest.
Arguments:
- queries: bfloat16 [32768, 4096], P(('dp', 'context', 'ulysses')), parts along dimension 0, may hold values from -5 to 5
- keys: bfloat16 [32768, 512], P(('dp', 'context', 'ulysses')), parts along dimension 0, may hold values from -5 to 5
- values: bfloat16 [32768, 512], P(('dp', 'context', 'ulysses')), parts along dimension 0, may hold values from -6 to 6
- segments: int32 [32768], P(('dp', 'context')), parts along dimension 0, may hold values from 0 to 63, never falling along the last dimension, each value on 1 to 4096 neighbouring positions
- feat_q: bfloat16 [32, 128, 128], P('ulysses'), may hold values from -2 to 2
- feat_k: bfloat16 [4, 128, 128], P('ulysses'), may hold values from -2 to 2
Outputs:
- error: bfloat16 [32768, 4096], P(('dp', 'context'), 'ulysses'), parts along dimension 0
- grad_keys: bfloat16 [32768, 512], P(('dp', 'context'), 'ulysses'), parts along dimension 0
- grad_feat_q: float32 [64, 128, 128], P(('dp', 'ulysses')), parts along dimension 0
- grad_feat_k: float32 [8, 128, 128], P(('dp', 'ulysses')), parts along dimension 0
There are 2 independent parts, one for each index of `dp`. A program takes and returns all parts, laid end to end along the dimension named above; an argument that names none is the same for every part. Nothing has to cross between parts.
Inputs may be any that keep to these rules, and one draw needn't show every extreme that they name: `segments`: document numbers never fall along the sequence; each document covers 1 to 4096 positions, and one covers exactly 4096.
All inputs are finite; a program needn't handle non-finite values.
Results may differ from a plain program's by a relative error of at most 0.015.
Values may be sent and summed in bfloat16 or wider, within the bound.
A program may use at most 128 MiB of HBM per device.

v0:
```python
import math
import jax
import jax.numpy as jnp
from jax import lax
from jax.sharding import PartitionSpec as P

WIN = 128


def entering(value, axis, join, neutral, backward):
    count, mine = (lax.axis_size(axis), lax.axis_index(axis))
    pieces = jax.tree.map(lambda part: lax.all_gather(part, axis), value)
    if backward:
        pieces = jax.tree.map(lambda part: part[::-1], pieces)
        mine = count - 1 - mine
    so_far = jax.tree.map(
        lambda part, zero: jnp.full_like(part, 0) + jnp.asarray(zero, part.dtype), value, neutral
    )

    def lap(position, so_far):
        longer = join(so_far, jax.tree.map(lambda part: part[position], pieces))
        return jax.tree.map(lambda new, old: jnp.where(position < mine, new, old), longer, so_far)

    return lax.fori_loop(0, count - 1, lap, so_far)


def from_behind(block, axis, distance):
    devices = range(lax.axis_size(axis))
    route = [(i - distance, i) for i in devices if i - distance in devices]
    return lax.ppermute(block, axis, route)


def feature_map(pre):
    return jnp.where(pre > 0, pre + 1.0, jnp.exp(jnp.minimum(pre, 0.0)))


def feature_slope(pre):
    return jnp.where(pre > 0, 1.0, jnp.exp(jnp.minimum(pre, 0.0)))


def join_parts(earlier, later):
    empty_later = later[2] < 0
    keep = (earlier[2] == later[2]) | empty_later
    return (
        later[0] + jnp.where(keep, earlier[0], 0.0),
        later[1] + jnp.where(keep, earlier[1], 0.0),
        jnp.where(empty_later, earlier[2], later[2]),
    )


def widened(form, left, right):
    return jnp.einsum(form, left, right, preferred_element_type=jnp.float32)


def split_pair(whole):
    upper = whole.astype(jnp.bfloat16)
    lower = (whole - upper.astype(jnp.float32)).astype(jnp.bfloat16)
    return (upper, lower)


def paired(form, left, pair, pair_first):
    if pair_first:
        return widened(form, pair[0], left) + widened(form, pair[1], left)
    return widened(form, left, pair[0]) + widened(form, left, pair[1])


def on_device(queries, keys, values, segments, feat_q, feat_k):
    query_all, key_all, value_all = (
        lax.all_to_all(queries, "ulysses", split_axis=1, concat_axis=0, tiled=True),
        lax.all_to_all(keys, "ulysses", split_axis=1, concat_axis=0, tiled=True),
        lax.all_to_all(values, "ulysses", split_axis=1, concat_axis=0, tiled=True),
    )
    length = query_all.shape[0]
    kv_heads, width, feats = feat_k.shape
    group = feat_q.shape[0] // kv_heads
    query_heads = query_all.reshape(length, kv_heads, group, width)
    key_heads = key_all.reshape(length, kv_heads, width)
    value_heads = value_all.reshape(length, kv_heads, width)
    pre_q = widened("rgke,gkef->rgkf", query_heads, feat_q.reshape(kv_heads, group, width, feats))
    phi_q = feature_map(pre_q).astype(jnp.bfloat16)
    pre_k = widened("rge,gef->rgf", key_heads, feat_k)
    phi_k = feature_map(pre_k).astype(jnp.bfloat16)
    here = lax.axis_index("context")
    first_id = segments[0]
    last_id = segments[length - 1]
    tail_k = jnp.where((segments == last_id)[:, None, None], phi_k, jnp.zeros_like(phi_k))
    state_local = widened("rgf,rge->gfe", tail_k, value_heads)
    norm_local = jnp.sum(tail_k.astype(jnp.float32), axis=0)
    blank = (jnp.zeros_like(state_local), jnp.zeros_like(norm_local))
    state_in, norm_in, state_id = entering(
        (state_local, norm_local, last_id),
        "context",
        join_parts,
        (blank[0], blank[1], jnp.int32(-1)),
        False,
    )
    state_parts = split_pair(state_in)
    norm_parts = split_pair(norm_in)
    rim_keys, rim_values, rim_ids = from_behind(
        (key_heads[length - WIN :], value_heads[length - WIN :], segments[length - WIN :]),
        "context",
        1,
    )
    rim_ids = jnp.where(here > 0, rim_ids, -1)
    keys_ext = jnp.concatenate([rim_keys, key_heads], axis=0)
    values_ext = jnp.concatenate([rim_values, value_heads], axis=0)
    ids_ext = jnp.concatenate([rim_ids, segments], axis=0)
    place = jnp.arange(length)
    place_ext = jnp.arange(length + WIN) - WIN
    take_in = segments == state_id
    first_rows = segments == first_id
    inv_scale = 1.0 / math.sqrt(width)
    block = min(512, length)
    cot_state = blank[0]
    cot_norm = blank[1]
    linked = (place[None, :] <= place[:, None]) & (segments[None, :] == segments[:, None])
    linked = linked[:, None, None, :]
    scores = jnp.where(linked, widened("igkf,jgf->igkj", phi_q, phi_k), 0.0)
    carried = take_in[:, None, None]
    numer = widened("igkj,jge->igke", scores.astype(jnp.bfloat16), value_heads) + jnp.where(
        carried[..., None], paired("igkf,gfe->igke", phi_q, state_parts, False), 0.0
    )
    denom = jnp.sum(scores, axis=-1) + jnp.where(
        carried, paired("igkf,gf->igk", phi_q, norm_parts, False), 0.0
    )
    student = numer / denom[..., None]
    seen = (
        (place_ext[None, :] <= place[:, None])
        & (place_ext[None, :] > place[:, None] - WIN)
        & (ids_ext[None, :] == segments[:, None])
    )
    logits = jnp.where(
        seen[:, None, None, :],
        widened("igke,jge->igkj", query_heads, keys_ext) * inv_scale,
        -jnp.inf,
    )
    top = jnp.max(logits, axis=-1, keepdims=True)
    probs = jnp.exp(logits - top)
    teacher = (
        widened("igkj,jge->igke", probs.astype(jnp.bfloat16), values_ext)
        / jnp.sum(probs, axis=-1)[..., None]
    )
    gap = student - teacher
    errors = gap.astype(jnp.bfloat16).reshape(block, kv_heads * group * width)
    upstream = 32.0 * gap
    d_numer = (upstream / denom[..., None]).astype(jnp.bfloat16)
    d_denom = -jnp.sum(upstream * student, axis=-1) / denom
    d_scores = jnp.where(
        linked, widened("igke,jge->igkj", d_numer, value_heads) + d_denom[..., None], 0.0
    ).astype(jnp.bfloat16)
    d_phi_q_parts = widened("igkj,jgf->igkf", d_scores, phi_k) + jnp.where(
        carried[..., None],
        paired("gfe,igke->igkf", d_numer, state_parts, True)
        + d_denom[..., None] * norm_in[None, :, None, :],
        0.0,
    )
    d_phi_k = widened("igkj,igkf->jgf", d_scores, phi_q)
    head_rows = first_rows[:, None, None, None]
    cot_state = widened(
        "igkf,igke->gfe", jnp.where(head_rows, phi_q, jnp.zeros_like(phi_q)), d_numer
    )
    cot_norm = jnp.sum(jnp.where(head_rows, d_denom[..., None] * phi_q, 0.0), axis=(0, 2))
    back_state, back_norm, back_id = entering(
        (cot_state, cot_norm, first_id),
        "context",
        join_parts,
        (blank[0], blank[1], jnp.int32(-1)),
        True,
    )
    take_back = (segments == back_id)[:, None, None]
    back_parts = split_pair(back_state)
    d_phi_k = d_phi_k + jnp.where(
        take_back, paired("gfe,jge->jgf", value_heads, back_parts, True) + back_norm[None], 0.0
    )
    d_pre_k = (d_phi_k * feature_slope(pre_k)).astype(jnp.bfloat16)
    grad_keys = (
        widened("jgf,gef->jge", d_pre_k, feat_k)
        .astype(jnp.bfloat16)
        .reshape(length, kv_heads * width)
    )
    d_pre_q = (d_phi_q_parts * feature_slope(pre_q)).astype(jnp.bfloat16)
    grad_query_maps = widened("rgke,rgkf->gkef", query_heads, d_pre_q).reshape(
        kv_heads * group, width, feats
    )
    grad_key_maps = widened("rge,rgf->gef", key_heads, d_pre_k)
    grad_query_maps, grad_key_maps = (
        lax.psum(grad_query_maps.astype(jnp.bfloat16), "context").astype(jnp.float32),
        lax.psum(grad_key_maps.astype(jnp.bfloat16), "context").astype(jnp.float32),
    )
    scale = 1.0 / math.sqrt(length * lax.axis_size("context"))
    return (errors, grad_keys, grad_query_maps * scale, grad_key_maps * scale)


def solution(mesh):
    in_specs = (
        P(("dp", "context", "ulysses"), None),
        P(("dp", "context", "ulysses"), None),
        P(("dp", "context", "ulysses"), None),
        P(("dp", "context")),
        P("ulysses", None, None),
        P("ulysses", None, None),
    )
    out_specs = (
        P(("dp", "context"), "ulysses"),
        P(("dp", "context"), "ulysses"),
        P(("dp", "ulysses"), None, None),
        P(("dp", "ulysses"), None, None),
    )
    return jax.shard_map(
        on_device, mesh=mesh, in_specs=in_specs, out_specs=out_specs, check_vma=False
    )
```

profile of v0, /device:TPU:8, one launch (start us, length us, event | category | flops | bytes accessed | tf_op | source)
XLA Modules:
  0.0 722.6 jit_solution(18378612023101309730)
XLA Ops:
  7.2 1.1 copy.70
  9.1 5.4 all-to-all-start
  14.5 1.3 dynamic-slice
  15.8 1.9 fusion.127
  17.7 1.3 broadcast_compare_fusion.6
  19.1 1.7 copy.77
  20.7 4.8 all-to-all-start.2
  25.5 1.7 convert_reduce_fusion
  27.2 2.8 all-to-all-done.2
  30.9 1.1 copy.158
  32.0 4.9 all-to-all-start.1
  36.9 2.9 collective-permute-start.1
  40.7 23.7 %all-reduce.2 = (s32[32]{0:T(128)S(1)}, s32[32]{0:T(128)}) all-reduce(s32[32]{0:T(128)S(1)} %get-tuple-element.424, s32[32]{0:T(128)S(1)} %slice_dynamic-update-slice_fusion), channel_id=1, replica_groups=mesh['context'=32,'ulysses'=4,'dp'=2] {'context'}, use_global_device_ids=true, to_apply=%add | all-reduce | flops 64 | bytes 512
  66.4 1.4 collective-permute-start.2
  68.4 3.9 collective-permute-start
  72.3 37.9 %all-gather.4 = f32[32,1,128]{2,1,0:T(1,128)S(1)} all-gather(f32[1,1,128]{2,1,0:T(1,128)S(1)} %bitcast.397), channel_id=3, replica_groups=mesh['context'=32,'ulysses'=4,'dp'=2] {'context'}, dimensions={0}, use_global_device_ids=true | all-gather | bytes 16896 | tf_op jit(solution)/shard_map/all_gather | solution.py:12
  110.4 2.0 select_convert_fusion
  112.4 4.0 fusion.10
  116.5 1.8 fusion.9
  118.3 4.0 copy-done.1
  122.3 2.2 fusion.4
  124.5 107.3 %while.36 = (s32[]{:T(128)}, f32[1,128,128]{2,1,0:T(8,128)S(1)}, f32[1,128]{1,0:T(1,128)S(1)}, s32[]{:T(128)}, s32[]{:T(128)}, /*index=5*/f32[32,1,128,128]{3,2,...) while((s32[]{:T(128)}, f32[1,128,128]{2,1,0:T(8,128)S(1)}, ...), condition=%wide.region_2.3_spmd.clone, body=%wide.region_1.2_spmd.clone.sunk | while | flops 66057 | bytes 198336 | solution.py:24
  126.6 0.9 fusion.142
  130.0 0.9 fusion.142
  133.5 0.9 fusion.142
  140.4 0.9 fusion.142
  143.8 0.9 fusion.142
  147.3 0.9 fusion.142
  150.7 0.9 fusion.142
  154.2 0.9 fusion.142
  157.7 0.9 fusion.142
  164.6 0.9 fusion.142
  168.0 0.9 fusion.142
  171.5 0.9 fusion.142
  174.9 0.9 fusion.142
  178.4 0.9 fusion.142
  185.3 0.9 fusion.142
  188.8 0.9 fusion.142
  192.2 0.9 fusion.142
  232.3 1.9 fusion.51
  234.2 1.8 fusion.55
  236.0 1.8 fusion.57
  238.4 2.4 copy.112
  242.2 4.7 fusion.24
  246.9 1.3 slice-done.2
  248.2 4.8 multiply_reduce_fusion
  253.0 1.8 fusion.44
  254.8 1.7 fusion.19
  256.5 2.1 fusion.84
  259.1 5.2 fusion.39
  264.4 1.1 convolution_bitcast_fusion.1
  266.0 37.3 %all-gather.5 = f32[32,1,128]{2,1,0:T(1,128)S(1)} all-gather(f32[1,1,128]{2,1,0:T(1,128)S(1)} %bitcast.396), channel_id=5, replica_groups=mesh['context'=32,'ulysses'=4,'dp'=2] {'context'}, dimensions={0}, use_global_device_ids=true | all-gather | bytes 16896 | tf_op jit(solution)/shard_map/all_gather | solution.py:12
  303.3 2.3 copy.100
  305.6 101.9 %all-reduce.5.cloned.1.call-done = bf16[8,128,128]{1,2,0:T(8,128)(2,1)} async-done(((bf16[8,128,128]{1,2,0:T(8,128)(2,1)}), bf16[8,128,128]{1,2,0:T(8,128)(2,1)}) %all-reduce.5.cloned.1.call-update) | async-done | bytes 262160 | tf_op jit(solution)/shard_map/psum | solution.py:187
  407.4 1.0 convert_multiply_fusion
  408.4 1.0 copy.101
  409.4 76.1 %all-gather.11.cloned.1.call-done = f32[4096,128]{1,0:T(8,128)} async-done(((f32[128,128]{1,0:T(8,128)}), f32[4096,128]{1,0:T(8,128)}) %all-gather.11.cloned.1.call-update) | async-done | bytes 2097168 | tf_op jit(solution)/shard_map/all_gather | solution.py:12
  485.5 1.7 rev.9
  487.3 81.0 %while.37 = (s32[]{:T(128)}, f32[1,128,128]{2,1,0:T(8,128)S(1)}, f32[1,128]{1,0:T(1,128)S(1)}, s32[]{:T(128)}, s32[]{:T(128)}, /*index=5*/f32[32,1,128,128]{3,2,...) while((s32[]{:T(128)}, f32[1,128,128]{2,1,0:T(8,128)S(1)}, ...), condition=%wide.region_9.10_spmd.clone, body=%wide.region_8.9_spmd.clone.sunk | while | flops 66057 | bytes 198336 | solution.py:24
  568.3 1.1 fusion.79
  569.4 1.1 fusion.36
  570.5 3.7 fusion.41
  574.4 0.9 convolution_convert_fusion
  575.3 140.0 %psum.15 = bf16[1,128,128]{1,2,0:T(8,128)(2,1)S(1)} all-reduce(bf16[1,128,128]{1,2,0:T(8,128)(2,1)S(1)} %fusion.42), channel_id=1, replica_groups=mesh['context'=32,'ulysses'=4,'dp'=2] {'context'}, use_global_device_ids=true, to_apply=%region_11.12 | all-reduce | flops 16384 | bytes 65536 | tf_op jit(solution)/shard_map/psum | solution.py:188
  (264 shorter events, 60.1 us)
Async XLA Ops:
  7.2 103.3 %copy-start = (bf16[8,128,128]{2,1,0:T(8,128)(2,1)S(1)}, bf16[8,128,128]{2,1,0:T(8,128)(2,1)}, u32[]{:S(2)}) copy-start(bf16[8,128,128]{2,1,0:T(8,128)(2,1)} %param.14) | copy-start | bytes 786436
  7.2 23.7 %copy-start.13 = (bf16[128,4096]{1,0:T(8,128)(2,1)S(1)}, bf16[128,4096]{1,0:T(8,128)(2,1)}, u32[]{:S(2)}) copy-start(bf16[128,4096]{1,0:T(8,128)(2,1)} %param.10) | copy-start | bytes 3145732
  9.1 11.6 %all-to-all-start = ((bf16[128,4,128]{2,0,1:T(8,128)(2,1)}), bf16[128,4,128]{2,0,1:T(8,128)(2,1)S(1)}, u32[]{:S(2)}, u32[]{:S(2)}) async-start(bf16[128,4,128]{2,0,1:T(8,128)(2,1)} %copy.71), calls=%async_computation | async-start | bytes 262144 | tf_op jit(solution)/shard_map/all_to_all | solution.py:70
  20.7 95.7 %copy-start.11 = (bf16[128,4,128]{2,0,1:T(8,128)(2,1)}, bf16[128,4,128]{2,0,1:T(8,128)(2,1)S(1)}, u32[]{:S(2)}) copy-start(bf16[128,4,128]{2,0,1:T(8,128)(2,1)S(1)} %all-to-all-done) | copy-start | bytes 393220
  20.7 9.3 %all-to-all-start.2 = ((bf16[128,4,128]{0,2,1:T(8,128)(2,1)}), bf16[128,4,128]{0,2,1:T(8,128)(2,1)S(1)}, u32[]{:S(2)}, u32[]{:S(2)}) async-start(bf16[128,4,128]{0,2,1:T(8,128)(2,1)} %bitcast.15), calls=%async_computation.2 | async-start | bytes 262144 | tf_op jit(solution)/shard_map/all_to_all | solution.py:71
  25.5 98.9 %all-gather.9.cloned.1.call-start = ((), (), s32[]{:S(2)}) async-start(), calls=%async_computation.4 | async-start | bytes 2162688 | tf_op jit(solution)/shard_map/all_gather | solution.py:12
  27.2 85.2 %copy-start.16 = (bf16[128,512]{1,0:T(8,128)(2,1)}, bf16[128,512]{1,0:T(8,128)(2,1)S(1)}, u32[]{:S(2)}) copy-start(bf16[128,512]{1,0:T(8,128)(2,1)S(1)} %get-tuple-element.417) | copy-start | bytes 393220
  30.0 37.7 %copy-start.9 = (bf16[128,4,128]{0,2,1:T(8,128)(2,1)}, bf16[128,4,128]{0,2,1:T(8,128)(2,1)S(1)}, u32[]{:S(2)}) copy-start(bf16[128,4,128]{0,2,1:T(8,128)(2,1)S(1)} %all-to-all-done.2) | copy-start | bytes 393220
  30.9 6.0 copy-start.19
  32.0 78.2 %all-to-all-start.1 = ((bf16[128,4,1024]{2,0,1:T(8,128)(2,1)}), bf16[128,4,1024]{2,0,1:T(8,128)(2,1)S(1)}, u32[]{:S(2)}, u32[]{:S(2)}) async-start(bf16[128,4,1024]{2,0,1:T(8,128)(2,1)} %bitcast.364), calls=%async_computation.1 | async-start | bytes 2097152 | tf_op jit(solution)/shard_map/all_to_all | solution.py:69
  36.9 370.5 %all-reduce.5.cloned.1.call-start = ((), (), s32[]{:S(2)}) async-start(), calls=%async_computation.3 | async-start | bytes 524288 | tf_op jit(solution)/shard_map/psum | solution.py:187
  36.9 27.5 %collective-permute-start.1 = (s32[128]{0:T(128)S(1)}, s32[128]{0:T(128)S(1)}, u32[]{:S(2)}, u32[]{:S(2)}) collective-permute-start(s32[128]{0:T(128)S(1)} %slice.24), channel_id=1, source_target_pairs={{0,8},{8,16},{16,24},{24,32},{32,40},{40,48},{48,56},{56,64},{64,7... | collective-permute-start | bytes 1544 | tf_op jit(solution)/shard_map/ppermute | solution.py:30
  40.7 71.7 %copy-start.14 = (pred[512,512]{0,1:T(8,128)(4,1)}, pred[512,512]{0,1:T(8,128)(4,1)S(1)}, u32[]{:S(2)}) copy-start(pred[512,512]{0,1:T(8,128)(4,1)S(1)} %fusion.66) | copy-start | bytes 786436
  64.8 53.4 %copy-start.7 = (pred[512,640]{0,1:T(8,128)(4,1)}, pred[512,640]{0,1:T(8,128)(4,1)S(1)}, u32[]{:S(2)}) copy-start(pred[512,640]{0,1:T(8,128)(4,1)S(1)} %fusion.31) | copy-start | bytes 983044
  66.4 50.1 %collective-permute-start.2 = (bf16[128,1,128]{2,0,1:T(8,128)(2,1)S(1)}, bf16[128,1,128]{2,0,1:T(8,128)(2,1)S(1)}, u32[]{:S(2)}, u32[]{:S(2)}) collective-permute-start(bf16[128,1,128]{2,0,1:T(8,128)(2,1)S(1)} %slice_bitcast_fusion), channel_id=1, source_target_pairs={{0,8},{8,16},{16,24},{24,32},{32,40},{40,48},{48,56},{56,64},{64,7... | collective-permute-start | bytes 98312 | tf_op jit(solution)/shard_map/ppermute | solution.py:30
  68.4 178.5 %collective-permute-start = (bf16[128,1,128]{0,2,1:T(8,128)(2,1)}, bf16[128,1,128]{0,2,1:T(8,128)(2,1)}, u32[]{:S(2)}, u32[]{:S(2)}) collective-permute-start(bf16[128,1,128]{0,2,1:T(8,128)(2,1)} %slice_bitcast_fusion.1), channel_id=1, source_target_pairs={{0,8},{8,16},{16,24},{24,32},{32,40},{40,48},{48,56},{56,64},{64,7... | collective-permute-start | bytes 98312 | tf_op jit(solution)/shard_map/ppermute | solution.py:30
  110.4 6.1 copy-start.2
  118.3 4.0 copy-start.1
  238.4 8.5 %slice-start = ((s8[10485760]{0:T(1024)(128)(4,1)}), s8[2097152]{0:T(1024)(128)(4,1)S(1)}, s32[]{:S(2)}) async-start(s8[10485760]{0:T(1024)(128)(4,1)} %bitcast.377), calls=%async_computation.6 | async-start | bytes 4194304
  242.1 4.8 slice-start.1
  242.1 6.0 slice-start.2
  242.1 6.0 copy-start.8
  242.1 6.0 copy-start.18
  253.0 3.5 copy-start.5
  253.0 1.8 copy-start.10
  253.0 1.8 copy-start.15
  254.8 1.7 copy-start.17
  256.5 2.6 copy-start.4
  256.5 2.6 copy-start.3
  259.1 5.3 copy-start.6
  264.3 1.2 copy-start.21
  264.3 221.2 %all-gather.11.cloned.1.call-start = ((), (), s32[]{:S(2)}) async-start(), calls=%async_computation.5 | async-start | bytes 2162688 | tf_op jit(solution)/shard_map/all_gather | solution.py:12
  570.5 3.7 copy-start.12
  570.5 3.9 copy-start.20
Sparse Core Ops, SparseCore 0:
  31.0 79.2 all-gather.8
  264.4 142.9 all-reduce.4
  410.6 74.8 all-gather.10
where the time goes:
time: 727 us; the launch traced here: 723 us
  blocking collectives  239 us (33%)
  waiting for transfers between devices  181 us (25%)
  loops' own time  123 us (17%)
  local copies, waits for them, and re-layouts  61.8 us (9%)
  matrix products  44.6 us (6%)
  other arithmetic  35.4 us (5%)
  starting transfers between devices  23.4 us (3%)
  between operations  14.2 us (2%)
    psum x1, blocking collectives, on_device(): lax.psum(grad_key_maps.astype(jnp.bfloat16), 'context').astype(jnp.float32)  140 us
    another operation x2, loops' own time, entering(): return lax.fori_loop(0, count - 1, lap, so_far)  123 us
    psum x1, waiting for transfers between devices, on_device(): lax.psum(grad_query_maps.astype(jnp.bfloat16), 'context')  102 us
    all_gather x2, waiting for transfers between devices, entering(): pieces = jax.tree.map(lambda part: lax.all_gather(part, axis), value)  76.1 us
    all_gather x2, blocking collectives, entering(): pieces = jax.tree.map(lambda part: lax.all_gather(part, axis), value)  75.2 us
    dot_general x21, matrix products, widened(): return jnp.einsum(form, left, right, preferred_element_type=jnp.float32)  44.6 us
    dynamic_slice x62, local copies, waits for them, and re-layouts, lap(): longer = join(so_far, jax.tree.map(lambda part: part[position], pieces))  36.4 us
    select_n x124, other arithmetic, lap(): jnp.where(position < mine, new, old)  28.5 us
  transfers between devices with their start and end apart: 9, of which 3 were waited for; matrix products, arithmetic and copies ran while one was open for 12% of the time, Pallas kernels for 0%

commit v1 on v0

--- a/solution.py
+++ b/solution.py
@@ -5,6 +5,12 @@
 from jax.sharding import PartitionSpec as P
 
 WIN = 128
+
+
+def name_region(frame, bus_axis):
+    now = lax.all_gather(frame, axis_name=bus_axis)
+    near = jnp.sum(now, 0)
+    return near
 
 
 def entering(value, axis, join, neutral, backward):
@@ -184,7 +190,7 @@
     )
     grad_key_maps = widened("rge,rgf->gef", key_heads, d_pre_k)
     grad_query_maps, grad_key_maps = (
-        lax.psum(grad_query_maps.astype(jnp.bfloat16), "context").astype(jnp.float32),
+        name_region(grad_query_maps.astype(jnp.bfloat16), "context").astype(jnp.float32),
         lax.psum(grad_key_maps.astype(jnp.bfloat16), "context").astype(jnp.float32),
     )
     scale = 1.0 / math.sqrt(length * lax.axis_size("context"))

time: 727 us -> 580 us (0.80)
  waiting for transfers between devices: 181 us -> 26.1 us
    psum x1 -> x0, waiting for transfers between devices: 102 us -> none  [on_device(): lax.psum(grad_query_maps.astype(jnp.bfloat16), 'context')]
    all_gather x2, waiting for transfers between devices: 76.1 us -> 23.2 us  [entering(): pieces = jax.tree.map(lambda part: lax.all_gather(part, axis), value)]
    unnamed x60 -> x51, local copies, waits for them, and re-layouts: 14.8 us -> 12.7 us
  transfers between devices with their start and end apart: 9 -> 9, of which waited for: 3 -> 2; matrix products, arithmetic and copies ran while one was open for 12% -> 22% of each run, Pallas kernels for 0% -> 0%
where the time goes in v1:
time: 580 us; the launch traced here: 576 us
  blocking collectives  239 us (41%)
  loops' own time  124 us (21%)
  local copies, waits for them, and re-layouts  61.9 us (11%)
  matrix products  49.3 us (8%)
  other arithmetic  39.1 us (7%)
  waiting for transfers between devices  26.1 us (4%)
  starting transfers between devices  23.2 us (4%)
  between operations  14.2 us (2%)
    psum x1, blocking collectives, on_device(): lax.psum(grad_key_maps.astype(jnp.bfloat16), 'context').astype(jnp.float32)  140 us
    another operation x2, loops' own time, entering(): return lax.fori_loop(0, count - 1, lap, so_far)  124 us
    all_gather x2, blocking collectives, entering(): pieces = jax.tree.map(lambda part: lax.all_gather(part, axis), value)  75.3 us
    dot_general x21, matrix products, widened(): return jnp.einsum(form, left, right, preferred_element_type=jnp.float32)  49.3 us
    dynamic_slice x62, local copies, waits for them, and re-layouts, lap(): longer = join(so_far, jax.tree.map(lambda part: part[position], pieces))  36.4 us
    select_n x124, other arithmetic, lap(): jnp.where(position < mine, new, old)  28.4 us
    unnamed x1, blocking collectives  23.6 us
    all_gather x2, waiting for transfers between devices, entering(): pieces = jax.tree.map(lambda part: lax.all_gather(part, axis), value)  23.2 us
  transfers between devices with their start and end apart: 9, of which 2 were waited for; matrix products, arithmetic and copies ran while one was open for 22% of the time, Pallas kernels for 0%

profile of v1, /device:TPU:8, one launch (start us, length us, event | category | flops | bytes accessed | tf_op | source)
XLA Modules:
  0.0 576.4 jit_solution(139579222113430922)
XLA Ops:
  7.2 1.1 copy.68
  9.1 5.4 all-to-all-start
  14.5 1.3 dynamic-slice
  15.8 2.0 fusion.127
  17.8 1.3 broadcast_compare_fusion.6
  19.1 1.7 copy.75
  20.8 4.8 all-to-all-start.2
  25.6 1.7 convert_reduce_fusion
  27.3 2.8 all-to-all-done.2
  31.0 1.1 copy.159
  32.1 4.9 all-to-all-start.1
  37.0 2.9 collective-permute-start.1
  40.9 23.6 %all-reduce.2 = (s32[32]{0:T(128)S(1)}, s32[32]{0:T(128)}) all-reduce(s32[32]{0:T(128)S(1)} %get-tuple-element.424, s32[32]{0:T(128)S(1)} %slice_dynamic-update-slice_fusion), channel_id=1, replica_groups=mesh['context'=32,'ulysses'=4,'dp'=2] {'context'}, use_global_device_ids=true, to_apply=%add | all-reduce | flops 64 | bytes 512
  65.8 1.4 collective-permute-start.2
  67.2 3.8 collective-permute-start
  71.0 38.0 %all-gather.5 = f32[32,1,128]{2,1,0:T(1,128)S(1)} all-gather(f32[1,1,128]{2,1,0:T(1,128)S(1)} %bitcast.397), channel_id=3, replica_groups=mesh['context'=32,'ulysses'=4,'dp'=2] {'context'}, dimensions={0}, use_global_device_ids=true | all-gather | bytes 16896 | tf_op jit(solution)/shard_map/all_gather | solution.py:18
  109.3 2.0 select_convert_fusion
  111.3 4.0 fusion.10
  115.4 1.8 fusion.9
  117.2 4.0 copy-done.1
  121.2 2.2 fusion.4
  123.4 107.2 %while.36 = (s32[]{:T(128)}, f32[1,128,128]{2,1,0:T(8,128)S(1)}, f32[1,128]{1,0:T(1,128)S(1)}, s32[]{:T(128)}, s32[]{:T(128)}, /*index=5*/f32[32,1,128,128]{3,2,...) while((s32[]{:T(128)}, f32[1,128,128]{2,1,0:T(8,128)S(1)}, ...), condition=%wide.region_2.3_spmd.clone, body=%wide.region_1.2_spmd.clone.sunk | while | flops 66057 | bytes 198336 | solution.py:30
  125.5 0.9 fusion.142
  128.9 0.9 fusion.142
  132.4 0.9 fusion.142
  135.8 0.9 fusion.142
  139.3 0.9 fusion.142
  142.7 0.9 fusion.142
  146.2 0.9 fusion.142
  149.6 0.9 fusion.142
  153.1 0.9 fusion.142
  156.5 0.9 fusion.142
  160.0 0.9 fusion.142
  163.4 0.9 fusion.142
  166.9 0.9 fusion.142
  170.3 0.9 fusion.142
  173.8 0.9 fusion.142
  177.2 0.9 fusion.142
  230.6 1.9 fusion.53
  232.5 1.9 fusion.51
  234.4 1.8 fusion.55
  236.1 1.8 fusion.57
  237.9 2.2 copy.111
  240.1 2.2 copy.112
  243.0 4.5 fusion.24
  247.5 8.3 %multiply_reduce_fusion = (f32[512,8]{0,1:T(8,128)S(1)}, bf16[512,1,8,128]{0,3,2,1:T(8,128)(2,1)S(1)}, bf16[512,1,8,128]{0,3,2,1:T(8,128)(2,1)}) fusion(f32[512,1,8,128]{0,3,2,1:T(8,128)S(1)} %fusion.24, f32[512,8]{0,1:T(8,128)S(1)} %fusion.105, f32[512,8]{0,1:T(8,128)S(1)} %fusion.4, f32[640,512,8]{1,0,2:T(8,128)} %copy-done.1, ...), kind=kOutput, calls=%fused_computation.42 | convolution fusion | flops 686092288 | bytes 15237120 | tf_op jit(solution)/shard_map/igkj,jge->igke/dot_general | solution.py:58
  255.9 1.1 convolution_bitcast_fusion.1
  257.0 1.8 fusion.44
  258.8 1.7 fusion.19
  260.5 2.5 fusion.84
  263.1 4.8 fusion.39
  267.9 1.9 copy.98
  270.3 37.3 %all-gather.6 = f32[32,1,128]{2,1,0:T(1,128)S(1)} all-gather(f32[1,1,128]{2,1,0:T(1,128)S(1)} %bitcast.396), channel_id=5, replica_groups=mesh['context'=32,'ulysses'=4,'dp'=2] {'context'}, dimensions={0}, use_global_device_ids=true | all-gather | bytes 16896 | tf_op jit(solution)/shard_map/all_gather | solution.py:18
  307.6 1.5 copy.100
  309.2 23.2 %all-gather.13.cloned.1.call-done = f32[4096,128]{1,0:T(8,128)} async-done(((f32[128,128]{1,0:T(8,128)}), f32[4096,128]{1,0:T(8,128)}) %all-gather.13.cloned.1.call-update) | async-done | bytes 2097168 | tf_op jit(solution)/shard_map/all_gather | solution.py:18
  332.4 1.7 rev.9
  334.1 81.1 %while.37 = (s32[]{:T(128)}, f32[1,128,128]{2,1,0:T(8,128)S(1)}, f32[1,128]{1,0:T(1,128)S(1)}, s32[]{:T(128)}, s32[]{:T(128)}, /*index=5*/f32[32,1,128,128]{3,2,...) while((s32[]{:T(128)}, f32[1,128,128]{2,1,0:T(8,128)S(1)}, ...), condition=%wide.region_9.10_spmd.clone, body=%wide.region_8.9_spmd.clone.sunk | while | flops 66057 | bytes 198336 | solution.py:30
  415.3 1.1 fusion.79
  416.3 1.1 fusion.36
  417.5 3.7 fusion.41
  421.4 140.1 %psum.7 = bf16[1,128,128]{1,2,0:T(8,128)(2,1)S(1)} all-reduce(bf16[1,128,128]{1,2,0:T(8,128)(2,1)S(1)} %fusion.42), channel_id=1, replica_groups=mesh['context'=32,'ulysses'=4,'dp'=2] {'context'}, use_global_device_ids=true, to_apply=%region_11.12 | all-reduce | flops 16384 | bytes 65536 | tf_op jit(solution)/shard_map/psum | solution.py:194
  562.2 0.9 convolution_convert_fusion
  563.1 5.5 reduce_sum.62
  568.9 1.0 copy.101
  (256 shorter events, 57.7 us)
Async XLA Ops:
  7.2 102.1 %copy-start = (bf16[8,128,128]{2,1,0:T(8,128)(2,1)S(1)}, bf16[8,128,128]{2,1,0:T(8,128)(2,1)}, u32[]{:S(2)}) copy-start(bf16[8,128,128]{2,1,0:T(8,128)(2,1)} %param.14) | copy-start | bytes 786436
  7.2 23.8 %copy-start.9 = (bf16[128,4096]{1,0:T(8,128)(2,1)S(1)}, bf16[128,4096]{1,0:T(8,128)(2,1)}, u32[]{:S(2)}) copy-start(bf16[128,4096]{1,0:T(8,128)(2,1)} %param.10) | copy-start | bytes 3145732
  9.1 11.7 %all-to-all-start = ((bf16[128,4,128]{2,0,1:T(8,128)(2,1)}), bf16[128,4,128]{2,0,1:T(8,128)(2,1)S(1)}, u32[]{:S(2)}, u32[]{:S(2)}) async-start(bf16[128,4,128]{2,0,1:T(8,128)(2,1)} %copy.69), calls=%async_computation | async-start | bytes 262144 | tf_op jit(solution)/shard_map/all_to_all | solution.py:76
  20.8 94.6 %copy-start.7 = (bf16[128,4,128]{2,0,1:T(8,128)(2,1)}, bf16[128,4,128]{2,0,1:T(8,128)(2,1)S(1)}, u32[]{:S(2)}) copy-start(bf16[128,4,128]{2,0,1:T(8,128)(2,1)S(1)} %all-to-all-done) | copy-start | bytes 393220
  20.8 9.3 %all-to-all-start.2 = ((bf16[128,4,128]{0,2,1:T(8,128)(2,1)}), bf16[128,4,128]{0,2,1:T(8,128)(2,1)S(1)}, u32[]{:S(2)}, u32[]{:S(2)}) async-start(bf16[128,4,128]{0,2,1:T(8,128)(2,1)} %bitcast.15), calls=%async_computation.2 | async-start | bytes 262144 | tf_op jit(solution)/shard_map/all_to_all | solution.py:77
  25.6 97.8 %all-gather.11.cloned.1.call-start = ((), (), s32[]{:S(2)}) async-start(), calls=%async_computation.3 | async-start | bytes 2162688 | tf_op jit(solution)/shard_map/all_gather | solution.py:18
  27.3 84.0 %copy-start.13 = (bf16[128,512]{1,0:T(8,128)(2,1)}, bf16[128,512]{1,0:T(8,128)(2,1)S(1)}, u32[]{:S(2)}) copy-start(bf16[128,512]{1,0:T(8,128)(2,1)S(1)} %get-tuple-element.417) | copy-start | bytes 393220
  30.1 37.1 %copy-start.5 = (bf16[128,4,128]{0,2,1:T(8,128)(2,1)}, bf16[128,4,128]{0,2,1:T(8,128)(2,1)S(1)}, u32[]{:S(2)}) copy-start(bf16[128,4,128]{0,2,1:T(8,128)(2,1)S(1)} %all-to-all-done.2) | copy-start | bytes 393220
  31.0 6.0 %copy-start.16 = (s32[512]{0:T(512)S(1)}, s32[512]{0:T(512)}, u32[]{:S(2)}) copy-start(s32[512]{0:T(512)} %param.13) | copy-start | bytes 6148
  32.1 77.0 %all-to-all-start.1 = ((bf16[128,4,1024]{2,0,1:T(8,128)(2,1)}), bf16[128,4,1024]{2,0,1:T(8,128)(2,1)S(1)}, u32[]{:S(2)}, u32[]{:S(2)}) async-start(bf16[128,4,1024]{2,0,1:T(8,128)(2,1)} %bitcast.365), calls=%async_computation.1 | async-start | bytes 2097152 | tf_op jit(solution)/shard_map/all_to_all | solution.py:75
  37.0 295.4 %all-gather.13.cloned.1.call-start = ((), (), s32[]{:S(2)}) async-start(), calls=%async_computation.4 | async-start | bytes 2162688 | tf_op jit(solution)/shard_map/all_gather | solution.py:18
  37.0 27.5 %collective-permute-start.1 = (s32[128]{0:T(128)S(1)}, s32[128]{0:T(128)S(1)}, u32[]{:S(2)}, u32[]{:S(2)}) collective-permute-start(s32[128]{0:T(128)S(1)} %slice.24), channel_id=1, source_target_pairs={{0,8},{8,16},{16,24},{24,32},{32,40},{40,48},{48,56},{56,64},{64,7... | collective-permute-start | bytes 1544 | tf_op jit(solution)/shard_map/ppermute | solution.py:36
  40.9 202.1 %copy-start.11 = (pred[512,512]{0,1:T(8,128)(4,1)}, pred[512,512]{0,1:T(8,128)(4,1)S(1)}, u32[]{:S(2)}) copy-start(pred[512,512]{0,1:T(8,128)(4,1)S(1)} %fusion.66) | copy-start | bytes 786436
  64.9 52.3 %copy-start.3 = (pred[512,640]{0,1:T(8,128)(4,1)}, pred[512,640]{0,1:T(8,128)(4,1)S(1)}, u32[]{:S(2)}) copy-start(pred[512,640]{0,1:T(8,128)(4,1)S(1)} %fusion.31) | copy-start | bytes 983044
  65.8 49.5 %collective-permute-start.2 = (bf16[128,1,128]{2,0,1:T(8,128)(2,1)S(1)}, bf16[128,1,128]{2,0,1:T(8,128)(2,1)S(1)}, u32[]{:S(2)}, u32[]{:S(2)}) collective-permute-start(bf16[128,1,128]{2,0,1:T(8,128)(2,1)S(1)} %slice_bitcast_fusion), channel_id=1, source_target_pairs={{0,8},{8,16},{16,24},{24,32},{32,40},{40,48},{48,56},{56,64},{64,7... | collective-permute-start | bytes 98312 | tf_op jit(solution)/shard_map/ppermute | solution.py:36
  67.2 180.2 %collective-permute-start = (bf16[128,1,128]{0,2,1:T(8,128)(2,1)S(1)}, bf16[128,1,128]{0,2,1:T(8,128)(2,1)}, u32[]{:S(2)}, u32[]{:S(2)}) collective-permute-start(bf16[128,1,128]{0,2,1:T(8,128)(2,1)S(1)} %slice_bitcast_fusion.1), channel_id=1, source_target_pairs={{0,8},{8,16},{16,24},{24,32},{32,40},{40,48},{48,56},{56,64},{64,7... | collective-permute-start | bytes 98312 | tf_op jit(solution)/shard_map/ppermute | solution.py:36
  117.2 4.0 copy-start.1
  237.9 5.0 copy-start.18
  243.0 4.5 copy-start.4
  243.0 4.5 copy-start.15
  256.9 306.2 %all-gather.15.cloned.1.call-start = ((), (), s32[]{:S(2)}) async-start(), calls=%async_computation.5 | async-start | bytes 8650752 | tf_op jit(solution)/shard_map/all_gather | solution.py:11
  257.0 1.8 copy-start.6
  257.0 1.8 copy-start.12
  258.8 1.7 copy-start.14
  260.5 2.6 copy-start.2
  263.1 6.7 %copy-start.19 = (s32[32]{0:T(128)S(1)}, s32[32]{0:T(128)}, u32[]{:S(2)}) copy-start(s32[32]{0:T(128)} %get-tuple-element.415) | copy-start | bytes 388
  267.9 39.7 %copy-start.10 = (bf16[512,1,8,128]{0,3,2,1:T(8,128)(2,1)S(1)}, bf16[512,1,8,128]{0,3,2,1:T(8,128)(2,1)}, u32[]{:S(2)}) copy-start(bf16[512,1,8,128]{0,3,2,1:T(8,128)(2,1)} %get-tuple-element.420) | copy-start | bytes 3145732
  417.4 3.8 copy-start.8
  417.4 144.8 %copy-start.17 = (bf16[1,128,128]{2,1,0:T(8,128)(2,1)S(1)}, bf16[1,128,128]{2,1,0:T(8,128)(2,1)}, u32[]{:S(2)}) copy-start(bf16[1,128,128]{2,1,0:T(8,128)(2,1)} %param.15) | copy-start | bytes 98308
Sparse Core Ops, SparseCore 0:
  31.1 79.4 all-gather.10
  257.1 75.2 all-gather.12
  335.0 95.0 all-gather.14
